TPU v7x, 256 devices: a whole 4x4x8 slice. The times are simulated.
256 devices in a mesh: seq: 64 (over z, y, core), ch: 4 (over x).
Axes of the slice: x: 4, y: 4, z: 8, core: 2. Of those that a mesh axis runs over, the one named last changes fastest.
Arguments:
- query_proj: bfloat16 [8192, 2048], P('seq', 'ch'), may hold values from -6 to 6
- key_proj: bfloat16 [8192, 2048], P('seq', 'ch'), may hold values from -6 to 6
- value_proj: bfloat16 [8192, 2048], P('seq', 'ch'), may hold values from -6 to 6
- short_filter: float32 [3, 3, 2048], P(None, None, 'ch'), may hold values from -3.5 to 3.5
- long_filter: float32 [8192, 2048], P('seq', 'ch'), may hold values from -0.0625 to 0.0625
- skip_gain: float32 [2048], P('ch'), may hold values from 0.5 to 1.5
- out_weight: bfloat16 [2048, 4096], P('ch'), may hold values from -0.125 to 0.125
- cotangent: bfloat16 [8192, 4096], P('seq', 'ch'), may hold values from -16 to 16
Outputs:
- layer_out: bfloat16 [8192, 4096], P('seq', 'ch')
- grad_query: float32 [8192, 2048], P('seq', 'ch')
- grad_key: float32 [8192, 2048], P('seq', 'ch')
- grad_value: float32 [8192, 2048], P('seq', 'ch')
- grad_short: float32 [3, 3, 2048], P(None, None, 'ch')
- grad_filter: float32 [8192, 2048], P('seq', 'ch')
- grad_skip: float32 [2048], P('ch')
- grad_w_out_t: float32 [4096, 2048], P('seq', 'ch')
All inputs are finite; a program needn't handle non-finite values.
Results may differ from a plain program's by a relative error of at most 0.011.
Values may be sent and summed in bfloat16 or wider, within the bound.
A program may use at most 128 MiB of HBM per device.

v0:
```python
import math
import jax
import jax.numpy as jnp
from jax import lax
from jax.sharding import PartitionSpec as P

exact_mode = lax.Precision.HIGHEST


def from_behind(shard, axis, by):
    size = lax.axis_size(axis)
    pairs = [(i, i + by) for i in range(size) if 0 <= i + by < size]
    return lax.ppermute(shard, axis, pairs)


def as_sent(shard):

    def short(part):
        return part.astype(jnp.bfloat16) if part.dtype == jnp.float32 else part

    return jax.tree.map(short, shard)


def split_lanes(merged, lanes):
    return tuple(
        (merged[..., start : start + lanes] for start in range(0, merged.shape[-1], lanes))
    )


def tables(rows_out, cols_in, period):
    row_index = lax.broadcasted_iota(jnp.int32, (rows_out, cols_in), 0)
    col_index = lax.broadcasted_iota(jnp.int32, (rows_out, cols_in), 1)
    phase_angle = (row_index * col_index % period).astype(jnp.float32) * (2.0 * math.pi / period)
    return (jnp.cos(phase_angle), jnp.sin(phase_angle))


def along_rows(factor, values):
    return jnp.tensordot(factor, values, axes=1, precision=exact_mode)


def rows_spectrum(signal, basis_pair):
    return (along_rows(basis_pair[0], signal), -along_rows(basis_pair[1], signal))


def rows_inverse(complex_pair, basis_pair):
    total = along_rows(basis_pair[0], complex_pair[0]) - along_rows(basis_pair[1], complex_pair[1])
    return total / basis_pair[0].shape[1]


def block_forward(complex_pair, basis_pair):
    cosine_part, sine_part = basis_pair
    real_part = along_rows(cosine_part, complex_pair[0]) + along_rows(sine_part, complex_pair[1])
    imag_part = along_rows(cosine_part, complex_pair[1]) - along_rows(sine_part, complex_pair[0])
    return (real_part, imag_part)


def block_inverse(complex_pair, basis_pair):
    cosine_part, sine_part = basis_pair
    norming = 1.0 / cosine_part.shape[1]
    real_part = along_rows(cosine_part, complex_pair[0]) - along_rows(sine_part, complex_pair[1])
    imag_part = along_rows(cosine_part, complex_pair[1]) + along_rows(sine_part, complex_pair[0])
    return (real_part * norming, imag_part * norming)


def complex_product(first_pair, second_pair):
    return (
        first_pair[0] * second_pair[0] - first_pair[1] * second_pair[1],
        first_pair[0] * second_pair[1] + first_pair[1] * second_pair[0],
    )


def conj_product(first_pair, second_pair):
    return (
        first_pair[0] * second_pair[0] + first_pair[1] * second_pair[1],
        first_pair[0] * second_pair[1] - first_pair[1] * second_pair[0],
    )


def on_device(
    query_proj, key_proj, value_proj, short_filter, long_filter, skip_gain, out_weight, cotangent
):
    block_rows = query_proj.shape[0]
    tap_count = short_filter.shape[1]
    block_count = lax.axis_size("seq")
    streams = jnp.stack([query_proj, key_proj, value_proj])
    earlier = from_behind(streams[:, block_rows - (tap_count - 1) :], "seq", 1)
    extended = jnp.concatenate([earlier, streams], axis=1).astype(jnp.float32)
    shifted = [
        extended[:, tap_count - 1 - offset : tap_count - 1 - offset + block_rows]
        for offset in range(tap_count)
    ]
    filtered = sum(
        (short_filter[:, offset][:, None, :] * shifted[offset] for offset in range(tap_count))
    )
    query_short, key_short, value_short = (filtered[0], filtered[1], filtered[2])
    product = key_short * value_short
    forward_basis = tables(2 * block_rows, block_rows, 2 * block_rows)
    full_basis = tables(2 * block_rows, 2 * block_rows, 2 * block_rows)
    half_basis = tables(block_rows, 2 * block_rows, 2 * block_rows)
    block_basis = tables(2 * block_count, block_count, 2 * block_count)
    return_basis = tables(block_count, 2 * block_count, 2 * block_count)
    input_pair = rows_spectrum(product, forward_basis)
    filter_pair = rows_spectrum(long_filter, forward_basis)
    lanes = product.shape[1]
    moved_data = split_lanes(
        lax.all_to_all(
            jnp.concatenate([input_pair[0], input_pair[1], filter_pair[0], filter_pair[1]], axis=1)[
                None
            ],
            "seq",
            split_axis=1,
            concat_axis=0,
            tiled=True,
        ),
        lanes,
    )
    input_spectrum = block_forward((moved_data[0], moved_data[1]), block_basis)
    filter_spectrum = block_forward((moved_data[2], moved_data[3]), block_basis)
    inverse_pair = block_inverse(complex_product(filter_spectrum, input_spectrum), return_basis)
    returned = split_lanes(
        lax.all_to_all(
            jnp.concatenate(inverse_pair, axis=-1), "seq", split_axis=0, concat_axis=1, tiled=True
        ),
        lanes,
    )
    folded = rows_inverse((returned[0][0], returned[1][0]), full_basis)
    carried = from_behind(folded[block_rows:], "seq", 1)
    convolved = folded[:block_rows] + carried
    mixed_seq = convolved + skip_gain * product
    gated_values = (query_short * mixed_seq).astype(jnp.bfloat16)
    partial_value = jnp.dot(gated_values, out_weight, preferred_element_type=jnp.float32)
    layer_out = lax.psum_scatter(partial_value, "ch", scatter_dimension=1, tiled=True).astype(
        jnp.bfloat16
    )
    full_cotangent = lax.all_gather(cotangent, "ch", axis=1, tiled=True)
    grad_gated = lax.dot_general(
        full_cotangent, out_weight, (((1,), (1,)), ((), ())), preferred_element_type=jnp.float32
    )
    weight_terms = lax.dot_general(
        full_cotangent, gated_values, (((0,), (0,)), ((), ())), preferred_element_type=jnp.float32
    )
    grad_mixed = grad_gated * query_short
    grad_query_short = grad_gated * mixed_seq
    following = from_behind(grad_mixed.astype(jnp.bfloat16), "seq", -1).astype(grad_mixed.dtype)
    spread = jnp.concatenate([grad_mixed, following], axis=0)
    grad_pair = rows_spectrum(spread, full_basis)
    moved_grad = split_lanes(
        lax.all_to_all(
            jnp.concatenate(grad_pair, axis=1)[None].astype(jnp.bfloat16),
            "seq",
            split_axis=1,
            concat_axis=0,
            tiled=True,
        ).astype(jnp.float32),
        lanes,
    )
    grad_spectrum = block_forward(moved_grad, block_basis)
    input_back = block_inverse(conj_product(filter_spectrum, grad_spectrum), return_basis)
    filter_back = block_inverse(conj_product(input_spectrum, grad_spectrum), return_basis)
    returned_grad = split_lanes(
        lax.all_to_all(
            as_sent(jnp.concatenate(input_back + filter_back, axis=-1)),
            "seq",
            split_axis=0,
            concat_axis=1,
            tiled=True,
        ),
        lanes,
    )
    conv_grad = rows_inverse((returned_grad[0][0], returned_grad[1][0]), half_basis)
    grad_filter = rows_inverse((returned_grad[2][0], returned_grad[3][0]), half_basis)
    grad_product = conv_grad + skip_gain * grad_mixed
    grad_streams = jnp.stack(
        [grad_query_short, grad_product * value_short, grad_product * key_short]
    )
    later_rows = from_behind(grad_streams[:, : tap_count - 1], "seq", -1)
    padded_grad = jnp.concatenate([grad_streams, later_rows], axis=1)
    grad_inputs = sum(
        (
            short_filter[:, offset][:, None, :] * padded_grad[:, offset : offset + block_rows]
            for offset in range(tap_count)
        )
    )
    short_terms = jnp.stack(
        [jnp.sum(grad_streams * shifted[offset], axis=1) for offset in range(tap_count)], axis=1
    )
    skip_terms = jnp.sum(grad_mixed * product, axis=0)
    channel_count = skip_terms.shape[0]
    sum_rows = short_terms.shape[0] * short_terms.shape[1] + 1
    padded_rows = -(-sum_rows // 8) * 8
    small_terms = jnp.concatenate(
        [
            short_terms.reshape(sum_rows - 1, channel_count),
            skip_terms[None],
            jnp.zeros((padded_rows - sum_rows, channel_count), jnp.float32),
        ]
    )
    weight_blocks = weight_terms.reshape(block_count, -1, channel_count)
    block_height = weight_blocks.shape[1]
    combined = jnp.concatenate(
        [weight_blocks, jnp.broadcast_to(small_terms, (block_count, padded_rows, channel_count))],
        axis=1,
    )
    reduced = lax.psum_scatter(
        combined.reshape(-1, channel_count), "seq", scatter_dimension=0, tiled=True
    )
    grad_w_out_t = reduced[:block_height]
    grad_short = reduced[block_height : block_height + sum_rows - 1].reshape(short_terms.shape)
    grad_skip = reduced[block_height + sum_rows - 1]
    return (
        layer_out,
        grad_inputs[0],
        grad_inputs[1],
        grad_inputs[2],
        grad_short,
        grad_filter,
        grad_skip,
        grad_w_out_t,
    )


def solution(mesh):
    in_specs = (
        P("seq", "ch"),
        P("seq", "ch"),
        P("seq", "ch"),
        P(None, None, "ch"),
        P("seq", "ch"),
        P("ch"),
        P("ch", None),
        P("seq", "ch"),
    )
    out_specs = (
        P("seq", "ch"),
        P("seq", "ch"),
        P("seq", "ch"),
        P("seq", "ch"),
        P(None, None, "ch"),
        P("seq", "ch"),
        P("ch"),
        P("seq", "ch"),
    )
    return jax.shard_map(
        on_device, mesh=mesh, in_specs=in_specs, out_specs=out_specs, check_vma=False
    )
```

profile of v0, /device:TPU:2, one launch (start us, length us, event | category | flops | bytes accessed | tf_op | source)
XLA Modules:
  0.0 450.7 jit_solution(9208655784076676578)
XLA Ops:
  8.7 1.7 collective-permute-start
  11.3 1.1 maximum_convert_fusion
  12.7 25.7 %all-gather.2.cloned.1.call-done = bf16[128,4096]{1,0:T(8,128)(2,1)} async-done(((bf16[128,1024]{1,0:T(8,128)(2,1)}), bf16[128,4096]{1,0:T(8,128)(2,1)}) %all-gather.2.cloned.1.call-update) | async-done | bytes 1048592 | tf_op jit(solution)/shard_map/all_gather | solution.py:135
  38.4 4.8 %multiply_reduce_fusion.3 = (f32[512]{0:T(512)S(1)}, f32[128,512]{1,0:T(8,128)S(1)}, f32[128,512]{1,0:T(8,128)S(1)}, f32[128,512]{1,0:T(8,128)}) fusion(f32[3,128,512]{2,1,0:T(8,128)S(1)} %multiply_add_fusion.3, bf16[128,4096]{1,0:T(8,128)(2,1)} %all-gather.2.cloned.1.call-done, bf16[512,4096]{1,0:T(8,128)(2,1)} %param.14), kind=kOutput, calls=%fused_computation.95 | convolution fusion | flops 537132544 | bytes 6817792 | tf_op jit(solution)/shard_map/dot_general | solution.py:136
  43.2 1.3 collective-permute-start.2
  44.5 1.9 collective-permute-done.2
  46.5 1.6 fusion.12
  48.1 1.6 fusion.13
  51.1 3.7 reduce.3
  54.8 1.1 reshape.83
  56.0 13.8 %all-to-all-start.2 = ((bf16[64,2,2048]{2,1,0:T(2,128)(2,1)}), bf16[64,2,2048]{2,1,0:T(2,128)(2,1)S(1)}, u32[]{:S(2)}, u32[]{:S(2)}) async-start(bf16[64,2,2048]{2,1,0:T(2,128)(2,1)} %reshape.83), calls=%async_computation.3 | async-start | bytes 1048576 | tf_op jit(solution)/shard_map/all_to_all | solution.py:148
  69.8 1.1 convolution_negate_fusion.1
  70.9 1.0 fusion.75
  71.9 1.1 convolution_negate_fusion.2
  73.0 1.1 fusion.77
  74.2 3.5 copy.39
  77.7 9.7 %all-to-all-done.2 = bf16[64,2,2048]{2,1,0:T(2,128)(2,1)S(1)} async-done(((bf16[64,2,2048]{2,1,0:T(2,128)(2,1)}), bf16[64,2,2048]{2,1,0:T(2,128)(2,1)S(1)}, u32[]{:S(2)}, u32[]{:S(2)}) %all-to-all-start.2) | async-done | bytes 524320 | tf_op jit(solution)/shard_map/all_to_all | solution.py:148
  88.2 5.8 %all-to-all-start = ((f32[1,256,2048]{2,0,1:T(1,128)}), f32[1,256,2048]{2,0,1:T(1,128)S(1)}, u32[]{:S(2)}, u32[]{:S(2)}) async-start(f32[1,256,2048]{2,0,1:T(1,128)} %copy.39), calls=%async_computation | async-start | bytes 4194304 | tf_op jit(solution)/shard_map/all_to_all | solution.py:106
  94.0 4.8 %reshape.84 = bf16[256,1,1024]{2,1,0:T(2,128)(2,1)} reshape(bf16[64,2,2048]{2,1,0:T(2,128)(2,1)} %copy-done.13) | data formatting | bytes 1048576
  98.9 5.1 %bitcast_reduce_fusion = bf16[256,1024]{1,0:T(8,128)(2,1)} fusion(bf16[256,1,1024]{2,1,0:T(2,128)(2,1)} %reshape.84), kind=kLoop, calls=%fused_computation.345 | loop fusion | bytes 1048576 | tf_op jit(solution)/shard_map/all_to_all | solution.py:148
  104.0 2.0 all_to_all.41
  106.0 1.2 fusion.301
  108.7 1.8 convolution_add_fusion
  110.5 1.7 convolution_subtract_fusion
  112.2 33.2 %all-to-all-done = f32[1,256,2048]{2,0,1:T(1,128)S(1)} async-done(((f32[1,256,2048]{2,0,1:T(1,128)}), f32[1,256,2048]{2,0,1:T(1,128)S(1)}, u32[]{:S(2)}, u32[]{:S(2)}) %all-to-all-start) | async-done | bytes 2097184 | tf_op jit(solution)/shard_map/all_to_all | solution.py:106
  145.4 6.8 %reduce = f32[256,2048]{1,0:T(8,128)} reduce(f32[1,256,2048]{2,0,1:T(1,128)S(1)} %all-to-all-done, f32[]{:T(128)} %constant.71), dimensions={0}, to_apply=%all_to_all.16.reduce_sub_computation | reduce | bytes 4194308 | tf_op jit(solution)/shard_map/all_to_all | solution.py:106
  152.2 2.0 all_to_all.17
  154.6 1.2 fusion.24
  155.8 1.2 fusion.20
  157.0 1.2 convolution_add_fusion.1
  158.2 1.2 convolution_subtract_fusion.1
  159.4 1.2 fusion.30
  160.6 1.2 fusion.26
  161.8 1.2 convolution_add_fusion.2
  163.0 2.8 multiply_add_fusion.1
  165.8 1.6 fusion.111
  167.4 1.0 fusion.115
  171.0 1.6 copy.44
  172.6 5.6 %all-to-all-start.1 = ((f32[64,4,1024]{2,1,0:T(4,128)}), f32[64,4,1024]{2,1,0:T(4,128)}, u32[]{:S(2)}, u32[]{:S(2)}) async-start(f32[64,4,1024]{2,1,0:T(4,128)} %copy.44), calls=%async_computation.1 | async-start | bytes 2097152 | tf_op jit(solution)/shard_map/all_to_all | solution.py:121
  184.4 1.8 copy.48
  186.2 20.8 %all-to-all-done.1 = f32[64,4,1024]{2,1,0:T(4,128)} async-done(((f32[64,4,1024]{2,1,0:T(4,128)}), f32[64,4,1024]{2,1,0:T(4,128)}, u32[]{:S(2)}, u32[]{:S(2)}) %all-to-all-start.1) | async-done | bytes 1048608 | tf_op jit(solution)/shard_map/all_to_all | solution.py:121
  206.9 5.8 %all-to-all-start.3 = ((bf16[64,4,2048]{2,1,0:T(4,128)(2,1)}), bf16[64,4,2048]{2,1,0:T(4,128)(2,1)S(1)}, u32[]{:S(2)}, u32[]{:S(2)}) async-start(bf16[64,4,2048]{2,1,0:T(4,128)(2,1)} %copy.48), calls=%async_computation.4 | async-start | bytes 2097152 | tf_op jit(solution)/shard_map/all_to_all | solution.py:161
  212.8 1.6 all_to_all.19
  214.4 1.6 fusion.19
  216.0 1.6 fusion.6
  218.5 2.9 collective-permute-start.1
  221.4 20.3 %all-to-all-done.3 = bf16[64,4,2048]{2,1,0:T(4,128)(2,1)S(1)} async-done(((bf16[64,4,2048]{2,1,0:T(4,128)(2,1)}), bf16[64,4,2048]{2,1,0:T(4,128)(2,1)S(1)}, u32[]{:S(2)}, u32[]{:S(2)}) %all-to-all-start.3) | async-done | bytes 1048608 | tf_op jit(solution)/shard_map/all_to_all | solution.py:161
  241.6 1.1 all_to_all.43
  242.8 1.8 fusion.36
  244.6 1.9 fusion.16
  246.5 1.0 multiply_bitcast_fusion.2
  247.7 2.1 fusion.303
  250.0 1.4 collective-permute-start.3
  251.4 4.5 %convolution_bitcast_fusion = f32[4096,512]{0,1:T(8,128)} fusion(bf16[128,512]{1,0:T(8,128)(2,1)S(1)} %get-tuple-element.36, bf16[128,4096]{1,0:T(8,128)(2,1)S(1)} %copy-done.10), kind=kOutput, calls=%fused_computation.1 | convolution fusion | flops 536870912 | bytes 9568256 | tf_op jit(solution)/shard_map/dot_general | solution.py:139
  255.9 9.1 %copy.49 = f32[4096,512]{1,0:T(8,128)} copy(f32[4096,512]{0,1:T(8,128)} %convolution_bitcast_fusion) | data formatting | bytes 16777216 | tf_op jit(solution)/shard_map/dot_general | solution.py:139
  265.1 1.4 multiply_reduce_fusion.2
  266.9 9.7 %pad_maximum_fusion = f32[64,80,512]{2,1,0:T(8,128)} fusion(f32[64,16,512]{2,1,0:T(8,128)S(1)} %broadcast_in_dim.18, f32[64,64,512]{2,1,0:T(8,128)} %bitcast.158), kind=kLoop, calls=%fused_computation | loop fusion | flops 2621440 | bytes 20971520 | tf_op jit(solution)/shard_map/concatenate | solution.py:200
  276.6 1.2 copy-done.18
  278.6 1.5 fusion.14
  280.1 0.9 slice_bitcast_fusion.8
  281.0 1.8 convert_element_type.109
  282.8 156.7 %reduce-scatter.5.cloned.1.call-done = f32[80,512]{1,0:T(8,128)} async-done(((f32[5120,512]{1,0:T(8,128)}), f32[80,512]{1,0:T(8,128)}) %reduce-scatter.5.cloned.1.call-update) | async-done | bytes 163856 | tf_op jit(solution)/shard_map/reduce_scatter | solution.py:204
  440.8 1.6 slice.163
  442.4 1.3 slice.162
  (92 shorter events, 19.1 us)
Async XLA Ops:
  7.2 62.6 %copy-start = (f32[128,512]{1,0:T(8,128)S(1)}, f32[128,512]{1,0:T(8,128)}, u32[]{:S(2)}) copy-start(f32[128,512]{1,0:T(8,128)} %param.12) | copy-start | bytes 786436
  7.2 31.2 %all-gather.2.cloned.1.call-start = ((), (), s32[]{:S(2)}) async-start(), calls=%async_computation.7 | async-start | bytes 1310720 | tf_op jit(solution)/shard_map/all_gather | solution.py:135
  8.7 2.6 collective-permute-start
  12.7 30.4 %copy-start.6 = (f32[3,128,512]{2,1,0:T(8,128)}, f32[3,128,512]{2,1,0:T(8,128)S(1)}, u32[]{:S(2)}) copy-start(f32[3,128,512]{2,1,0:T(8,128)S(1)} %multiply_add_fusion.3) | copy-start | bytes 2359300
  43.2 6.6 %copy-start.16 = (f32[128,512]{1,0:T(8,128)}, f32[128,512]{1,0:T(8,128)S(1)}, u32[]{:S(2)}) copy-start(f32[128,512]{1,0:T(8,128)S(1)} %get-tuple-element.12) | copy-start | bytes 786436
  43.2 3.2 collective-permute-start.2
  56.0 31.5 %all-to-all-start.2 = ((bf16[64,2,2048]{2,1,0:T(2,128)(2,1)}), bf16[64,2,2048]{2,1,0:T(2,128)(2,1)S(1)}, u32[]{:S(2)}, u32[]{:S(2)}) async-start(bf16[64,2,2048]{2,1,0:T(2,128)(2,1)} %reshape.83), calls=%async_computation.3 | async-start | bytes 1048576 | tf_op jit(solution)/shard_map/all_to_all | solution.py:148
  87.4 0.8 copy-start.13
  88.2 57.2 %all-to-all-start = ((f32[1,256,2048]{2,0,1:T(1,128)}), f32[1,256,2048]{2,0,1:T(1,128)S(1)}, u32[]{:S(2)}, u32[]{:S(2)}) async-start(f32[1,256,2048]{2,0,1:T(1,128)} %copy.39), calls=%async_computation | async-start | bytes 4194304 | tf_op jit(solution)/shard_map/all_to_all | solution.py:106
  160.5 2.4 copy-start.8
  160.6 2.4 copy-start.9
  165.8 3.5 copy-start.4
  172.6 34.3 %all-to-all-start.1 = ((f32[64,4,1024]{2,1,0:T(4,128)}), f32[64,4,1024]{2,1,0:T(4,128)}, u32[]{:S(2)}, u32[]{:S(2)}) async-start(f32[64,4,1024]{2,1,0:T(4,128)} %copy.44), calls=%async_computation.1 | async-start | bytes 2097152 | tf_op jit(solution)/shard_map/all_to_all | solution.py:121
  178.2 1.2 copy-start.3
  178.2 2.8 copy-start.12
  180.2 1.6 copy-start.5
  206.9 34.7 %all-to-all-start.3 = ((bf16[64,4,2048]{2,1,0:T(4,128)(2,1)}), bf16[64,4,2048]{2,1,0:T(4,128)(2,1)S(1)}, u32[]{:S(2)}, u32[]{:S(2)}) async-start(bf16[64,4,2048]{2,1,0:T(4,128)(2,1)} %copy.48), calls=%async_computation.4 | async-start | bytes 2097152 | tf_op jit(solution)/shard_map/all_to_all | solution.py:161
  212.8 68.2 %reduce-scatter.3.cloned.1.call-start = ((), (), s32[]{:S(2)}) async-start(), calls=%async_computation.6 | async-start | bytes 2621440 | tf_op jit(solution)/shard_map/reduce_scatter | solution.py:132
  217.7 0.8 copy-start.14
  217.7 26.8 %copy-start.17 = (f32[128,512]{1,0:T(8,128)S(1)}, f32[128,512]{1,0:T(8,128)}, u32[]{:S(2)}) copy-start(f32[128,512]{1,0:T(8,128)} %copy-done.16) | copy-start | bytes 786436
  217.7 26.8 %copy-start.20 = (f32[512]{0:T(512)S(1)}, f32[512]{0:T(512)}, u32[]{:S(2)}) copy-start(f32[512]{0:T(512)} %param.13) | copy-start | bytes 6148
  218.5 28.0 %copy-start.19 = (f32[128,512]{1,0:T(8,128)S(1)}, f32[128,512]{1,0:T(8,128)}, u32[]{:S(2)}) copy-start(f32[128,512]{1,0:T(8,128)} %get-tuple-element.42) | copy-start | bytes 786436
  218.5 28.0 %collective-permute-start.1 = (f32[128,512]{1,0:T(8,128)S(1)}, f32[128,512]{1,0:T(8,128)}, u32[]{:S(2)}, u32[]{:S(2)}) collective-permute-start(f32[128,512]{1,0:T(8,128)S(1)} %slice.148), channel_id=1, source_target_pairs={{0,4},{4,8},{8,12},{12,16},{16,20},{20,24},{24,28},{28,32},{32,36}... | collective-permute-start | bytes 786440 | tf_op jit(solution)/shard_map/ppermute | solution.py:13
  221.4 25.1 %copy-start.15 = (f32[256,512]{1,0:T(8,128)S(1)}, f32[256,512]{1,0:T(8,128)}, u32[]{:S(2)}) copy-start(f32[256,512]{1,0:T(8,128)} %copy-done.14) | copy-start | bytes 1572868
  242.8 4.8 %copy-start.7 = (f32[3,128,512]{2,1,0:T(8,128)S(1)}, f32[3,128,512]{2,1,0:T(8,128)}, u32[]{:S(2)}) copy-start(f32[3,128,512]{2,1,0:T(8,128)} %copy-done.6) | copy-start | bytes 2359300
  244.5 3.1 copy-start.2
  249.7 1.7 copy-start.10
  249.8 189.7 %reduce-scatter.5.cloned.1.call-start = ((), (), s32[]{:S(2)}) async-start(), calls=%async_computation.8 | async-start | bytes 10649600 | tf_op jit(solution)/shard_map/reduce_scatter | solution.py:204
  250.0 15.1 %collective-permute-start.3 = (f32[3,2,512]{2,1,0:T(2,128)S(1)}, f32[3,2,512]{2,1,0:T(2,128)S(1)}, u32[]{:S(2)}, u32[]{:S(2)}) collective-permute-start(f32[3,2,512]{2,1,0:T(2,128)S(1)} %slice.153), channel_id=1, source_target_pairs={{4,0},{8,4},{12,8},{16,12},{20,16},{24,20},{28,24},{32,28},{36,32}... | collective-permute-start | bytes 36872 | tf_op jit(solution)/shard_map/ppermute | solution.py:13
  276.6 1.2 copy-start.18
  277.9 2.2 copy-start.11
  277.9 165.8 %copy-start.1 = (f32[128,512]{1,0:T(8,128)S(1)}, f32[128,512]{1,0:T(8,128)}, u32[]{:S(2)}) copy-start(f32[128,512]{1,0:T(8,128)} %param.12) | copy-start | bytes 786436
Sparse Core Ops, SparseCore 0:
  9.8 28.5 all-gather.1
  249.9 27.6 reduce-scatter.2
  282.5 156.9 reduce-scatter.4
where the time goes:
time: 460 us; the launch traced here: 451 us
  waiting for transfers between devices  269 us (58%)
  matrix products  54.6 us (12%)
  local copies, waits for them, and re-layouts  46.4 us (10%)
  starting transfers between devices  38.5 us (8%)
  other arithmetic  27.3 us (6%)
  between operations  14.9 us (3%)
    reduce_scatter x1, waiting for transfers between devices, on_device(): lax.psum_scatter(combined.reshape(-1, channel_count), 'seq', scatter_dime...  157 us
    dot_general x36, matrix products, along_rows(): return jnp.tensordot(factor, values, axes=1, precision=exact_mode)  43.2 us
    all_to_all x1, waiting for transfers between devices, on_device(): lax.all_to_all(jnp.concatenate([input_pair[0], input_pair[1], filter_pair...  33.2 us
    all_gather x1, waiting for transfers between devices, on_device(): full_cotangent = lax.all_gather(cotangent, 'ch', axis=1, tiled=True)  25.7 us
    all_to_all x1, waiting for transfers between devices, on_device(): lax.all_to_all(jnp.concatenate(inverse_pair, axis=-1), 'seq', split_axis=...  20.8 us
    all_to_all x1, waiting for transfers between devices, on_device(): lax.all_to_all(as_sent(jnp.concatenate(input_back + filter_back, axis=-1)...  20.3 us
    all_to_all x1, starting transfers between devices, on_device(): lax.all_to_all(jnp.concatenate(grad_pair, axis=1)[None].astype(jnp.bfloat...  13.8 us
    all_to_all x1, waiting for transfers between devices, on_device(): lax.all_to_all(jnp.concatenate(grad_pair, axis=1)[None].astype(jnp.bfloat...  9.73 us
  transfers between devices with their start and end apart: 11, of which 7 were waited for; matrix products, arithmetic and copies ran while one was open for 16% of the time, Pallas kernels for 0%

commit v1 on v0

--- a/solution.py
+++ b/solution.py
@@ -5,6 +5,12 @@
 from jax.sharding import PartitionSpec as P
 
 exact_mode = lax.Precision.HIGHEST
+
+
+def joined_along(tiles, dim):
+    shape = list(tiles.shape[1:])
+    shape[dim] *= tiles.shape[0]
+    return jnp.moveaxis(tiles, 0, dim).reshape(shape)
 
 
 def from_behind(shard, axis, by):
@@ -132,7 +138,19 @@
     layer_out = lax.psum_scatter(partial_value, "ch", scatter_dimension=1, tiled=True).astype(
         jnp.bfloat16
     )
-    full_cotangent = lax.all_gather(cotangent, "ch", axis=1, tiled=True)
+    size_2 = lax.axis_size("ch")
+    pairs_2 = [(i_2, (i_2 + 1) % size_2) for i_2 in range(size_2)]
+    back = [(b, a) for a, b in pairs_2]
+    lower, upper = ([], [])
+    for lap in range(size_2 - 1):
+        if lap % 2 == 0:
+            lower.append(lax.ppermute(lower[-1] if lower else cotangent, "ch", pairs_2))
+        else:
+            upper.append(lax.ppermute(upper[-1] if upper else cotangent, "ch", back))
+    blocks = jnp.stack([*lower[::-1], cotangent, *upper])
+    shift = lax.axis_index("ch") - len(lower)
+    blocks = blocks[(jnp.arange(size_2) - shift) % size_2]
+    full_cotangent = joined_along(blocks, 1)
     grad_gated = lax.dot_general(
         full_cotangent, out_weight, (((1,), (1,)), ((), ())), preferred_element_type=jnp.float32
     )

time: 460 us -> 448 us (0.974)
  waiting for transfers between devices: 269 us -> 260 us
  starting transfers between devices: 38.5 us -> 45.2 us
  local copies, waits for them, and re-layouts: 46.4 us -> 40.6 us
    all_gather x1 -> x0, waiting for transfers between devices: 25.7 us -> none  [on_device(): full_cotangent = lax.all_gather(cotangent, 'ch', axis=1, tiled=True)]
    dot_general x1 -> x0, local copies, waits for them, and re-layouts: 9.14 us -> none  [on_device(): lax.dot_general(full_cotangent, gated_values, (((0,), (0,)), ((), ())), p...]
    ppermute x0 -> x3, waiting for transfers between devices: none -> 8.52 us  [the longest x2 8.51 us: on_device(): lower.append(lax.ppermute(lower[-1] if lower else cotangent, 'ch', pairs_2))]
    reduce_scatter x1, waiting for transfers between devices: 0.01 us -> 5.46 us  [on_device(): lax.psum_scatter(partial_value, 'ch', scatter_dimension=1, tiled=True)]
    unnamed x47 -> x51, local copies, waits for them, and re-layouts: 9.71 us -> 9.81 us
  transfers between devices with their start and end apart: 11 -> 13, of which waited for: 7 -> 9; matrix products, arithmetic and copies ran while one was open for 16% -> 14% of each run, Pallas kernels for 0% -> 0%
where the time goes in v1:
time: 448 us; the launch traced here: 443 us
  waiting for transfers between devices  260 us (58%)
  matrix products  54.6 us (12%)
  starting transfers between devices  45.2 us (10%)
  local copies, waits for them, and re-layouts  40.6 us (9%)
  other arithmetic  27.5 us (6%)
  between operations  15.3 us (3%)
    reduce_scatter x1, waiting for transfers between devices, on_device(): lax.psum_scatter(combined.reshape(-1, channel_count), 'seq', scatter_dime...  160 us
    dot_general x36, matrix products, along_rows(): return jnp.tensordot(factor, values, axes=1, precision=exact_mode)  43.2 us
    all_to_all x1, waiting for transfers between devices, on_device(): lax.all_to_all(jnp.concatenate([input_pair[0], input_pair[1], filter_pair...  33.1 us
    all_to_all x1, waiting for transfers between devices, on_device(): lax.all_to_all(jnp.concatenate(inverse_pair, axis=-1), 'seq', split_axis=...  20.8 us
    all_to_all x1, waiting for transfers between devices, on_device(): lax.all_to_all(as_sent(jnp.concatenate(input_back + filter_back, axis=-1)...  20.2 us
    all_to_all x1, starting transfers between devices, on_device(): lax.all_to_all(jnp.concatenate(grad_pair, axis=1)[None].astype(jnp.bfloat...  16.8 us
    unnamed x51, local copies, waits for them, and re-layouts  9.81 us
    all_to_all x1, waiting for transfers between devices, on_device(): lax.all_to_all(jnp.concatenate(grad_pair, axis=1)[None].astype(jnp.bfloat...  9.71 us
  transfers between devices with their start and end apart: 13, of which 9 were waited for; matrix products, arithmetic and copies ran while one was open for 14% of the time, Pallas kernels for 0%

profile of v1, /device:TPU:2, one launch (start us, length us, event | category | flops | bytes accessed | tf_op | source)
XLA Modules:
  0.0 443.1 jit_solution(5134162311349796524)
XLA Ops:
  7.2 1.6 collective-permute-start.2
  10.4 1.3 collective-permute-start
  12.6 1.2 maximum_convert_fusion
  13.8 1.7 collective-permute-done.2
  15.5 1.5 collective-permute-start.3
  17.3 6.8 %collective-permute-done.3 = bf16[128,1024]{1,0:T(8,128)(2,1)S(1)} collective-permute-done((bf16[128,1024]{1,0:T(8,128)(2,1)S(1)}, bf16[128,1024]{1,0:T(8,128)(2,1)S(1)}, u32[]{:S(2)}, u32[]{:S(2)}) %collective-permute-start.3) | collective-permute-done | bytes 262176 | tf_op jit(solution)/shard_map/ppermute | solution.py:147
  24.2 1.6 gather_fusion
  25.9 1.6 copy.50
  27.5 4.8 %multiply_reduce_fusion.3 = (f32[512]{0:T(512)S(1)}, f32[128,512]{1,0:T(8,128)S(1)}, f32[128,512]{1,0:T(8,128)S(1)}, f32[128,512]{1,0:T(8,128)}) fusion(f32[3,128,512]{2,1,0:T(8,128)S(1)} %multiply_add_fusion.3, bf16[128,4096]{0,1:T(8,128)(2,1)S(1)} %bitcast.166, bf16[512,4096]{1,0:T(8,128)(2,1)} %param.14), kind=kOutput, calls=%fused_computation.96 | convolution fusion | flops 537132544 | bytes 6817792 | tf_op jit(solution)/shard_map/dot_general | solution.py:154
  32.3 1.5 collective-permute-start.5
  33.8 1.7 collective-permute-done.5
  35.6 1.6 fusion.12
  37.2 1.6 fusion.13
  40.3 3.7 reduce.3
  44.0 1.1 reshape.143
  45.1 16.8 %all-to-all-start.2 = ((bf16[64,2,2048]{2,1,0:T(2,128)(2,1)}), bf16[64,2,2048]{2,1,0:T(2,128)(2,1)S(1)}, u32[]{:S(2)}, u32[]{:S(2)}) async-start(bf16[64,2,2048]{2,1,0:T(2,128)(2,1)} %reshape.143), calls=%async_computation.3 | async-start | bytes 1048576 | tf_op jit(solution)/shard_map/all_to_all | solution.py:166
  61.9 1.1 convolution_negate_fusion.1
  64.0 1.1 convolution_negate_fusion.2
  66.3 3.5 copy.44
  69.8 9.7 %all-to-all-done.2 = bf16[64,2,2048]{2,1,0:T(2,128)(2,1)S(1)} async-done(((bf16[64,2,2048]{2,1,0:T(2,128)(2,1)}), bf16[64,2,2048]{2,1,0:T(2,128)(2,1)S(1)}, u32[]{:S(2)}, u32[]{:S(2)}) %all-to-all-start.2) | async-done | bytes 524320 | tf_op jit(solution)/shard_map/all_to_all | solution.py:166
  80.4 5.8 %all-to-all-start = ((f32[1,256,2048]{2,0,1:T(1,128)}), f32[1,256,2048]{2,0,1:T(1,128)S(1)}, u32[]{:S(2)}, u32[]{:S(2)}) async-start(f32[1,256,2048]{2,0,1:T(1,128)} %copy.44), calls=%async_computation | async-start | bytes 4194304 | tf_op jit(solution)/shard_map/all_to_all | solution.py:112
  86.2 4.9 %reshape.144 = bf16[256,1,1024]{2,1,0:T(2,128)(2,1)} reshape(bf16[64,2,2048]{2,1,0:T(2,128)(2,1)} %copy-done.14) | data formatting | bytes 1048576
  91.1 5.1 %bitcast_reduce_fusion = bf16[256,1024]{1,0:T(8,128)(2,1)} fusion(bf16[256,1,1024]{2,1,0:T(2,128)(2,1)} %reshape.144), kind=kLoop, calls=%fused_computation.355 | loop fusion | bytes 1048576 | tf_op jit(solution)/shard_map/all_to_all | solution.py:166
  96.1 2.0 all_to_all.41
  98.2 1.2 fusion.305
  100.9 1.8 convolution_add_fusion
  102.7 1.7 convolution_subtract_fusion
  104.4 33.1 %all-to-all-done = f32[1,256,2048]{2,0,1:T(1,128)S(1)} async-done(((f32[1,256,2048]{2,0,1:T(1,128)}), f32[1,256,2048]{2,0,1:T(1,128)S(1)}, u32[]{:S(2)}, u32[]{:S(2)}) %all-to-all-start) | async-done | bytes 2097184 | tf_op jit(solution)/shard_map/all_to_all | solution.py:112
  137.5 6.8 %reduce = f32[256,2048]{1,0:T(8,128)} reduce(f32[1,256,2048]{2,0,1:T(1,128)S(1)} %all-to-all-done, f32[]{:T(128)} %constant.94), dimensions={0}, to_apply=%all_to_all.16.reduce_sub_computation | reduce | bytes 4194308 | tf_op jit(solution)/shard_map/all_to_all | solution.py:112
  144.3 2.0 all_to_all.17
  146.7 1.2 fusion.24
  147.9 1.2 fusion.20
  149.1 1.2 convolution_add_fusion.1
  150.3 1.2 convolution_subtract_fusion.1
  151.5 1.2 fusion.30
  152.7 1.2 fusion.26
  153.9 1.2 convolution_add_fusion.2
  155.1 2.8 multiply_add_fusion.1
  157.9 1.6 fusion.113
  163.0 1.6 copy.49
  164.7 5.6 %all-to-all-start.1 = ((f32[64,4,1024]{2,1,0:T(4,128)}), f32[64,4,1024]{2,1,0:T(4,128)}, u32[]{:S(2)}, u32[]{:S(2)}) async-start(f32[64,4,1024]{2,1,0:T(4,128)} %copy.49), calls=%async_computation.1 | async-start | bytes 2097152 | tf_op jit(solution)/shard_map/all_to_all | solution.py:127
  176.5 1.8 copy.54
  178.3 20.8 %all-to-all-done.1 = f32[64,4,1024]{2,1,0:T(4,128)} async-done(((f32[64,4,1024]{2,1,0:T(4,128)}), f32[64,4,1024]{2,1,0:T(4,128)}, u32[]{:S(2)}, u32[]{:S(2)}) %all-to-all-start.1) | async-done | bytes 1048608 | tf_op jit(solution)/shard_map/all_to_all | solution.py:127
  199.0 5.8 %all-to-all-start.3 = ((bf16[64,4,2048]{2,1,0:T(4,128)(2,1)}), bf16[64,4,2048]{2,1,0:T(4,128)(2,1)S(1)}, u32[]{:S(2)}, u32[]{:S(2)}) async-start(bf16[64,4,2048]{2,1,0:T(4,128)(2,1)} %copy.54), calls=%async_computation.4 | async-start | bytes 2097152 | tf_op jit(solution)/shard_map/all_to_all | solution.py:179
  204.9 1.6 all_to_all.19
  206.5 1.6 fusion.19
  208.1 1.6 fusion.6
  210.6 2.9 collective-permute-start.1
  213.5 20.2 %all-to-all-done.3 = bf16[64,4,2048]{2,1,0:T(4,128)(2,1)S(1)} async-done(((bf16[64,4,2048]{2,1,0:T(4,128)(2,1)}), bf16[64,4,2048]{2,1,0:T(4,128)(2,1)S(1)}, u32[]{:S(2)}, u32[]{:S(2)}) %all-to-all-start.3) | async-done | bytes 1048608 | tf_op jit(solution)/shard_map/all_to_all | solution.py:179
  233.7 1.1 all_to_all.43
  234.8 1.8 fusion.36
  236.7 1.9 fusion.16
  239.8 2.1 fusion.307
  242.1 1.4 collective-permute-start.6
  243.5 4.5 %fusion.55 = f32[64,64,512]{2,1,0:T(8,128)} fusion(bf16[64,64,128]{2,1,0:T(8,128)(2,1)S(1)} %bitcast.167, bf16[128,512]{1,0:T(8,128)(2,1)S(1)} %get-tuple-element.36), kind=kOutput, calls=%fused_computation.124 | convolution fusion | flops 536870912 | bytes 9568256 | tf_op jit(solution)/shard_map/dot_general | solution.py:157
  248.1 1.4 multiply_reduce_fusion.2
  249.9 9.6 %pad_maximum_fusion = f32[64,80,512]{2,1,0:T(8,128)} fusion(f32[64,16,512]{2,1,0:T(8,128)S(1)} %broadcast_in_dim.19, f32[64,64,512]{2,1,0:T(8,128)} %fusion.55), kind=kLoop, calls=%fused_computation.1 | loop fusion | flops 2621440 | bytes 20971520 | tf_op jit(solution)/shard_map/concatenate | solution.py:218
  259.6 1.2 copy-done.19
  261.5 1.5 fusion.14
  263.9 5.5 %reduce-scatter.3.cloned.1.call-done = f32[128,1024]{1,0:T(8,128)} async-done(((f32[128,4096]{1,0:T(8,128)}), f32[128,1024]{1,0:T(8,128)}) %reduce-scatter.3.cloned.1.call-update) | async-done | bytes 524304 | tf_op jit(solution)/shard_map/reduce_scatter | solution.py:138
  269.4 1.8 convert_element_type.109
  271.1 160.4 %reduce-scatter.5.cloned.1.call-done = f32[80,512]{1,0:T(8,128)} async-done(((f32[5120,512]{1,0:T(8,128)}), f32[80,512]{1,0:T(8,128)}) %reduce-scatter.5.cloned.1.call-update) | async-done | bytes 163856 | tf_op jit(solution)/shard_map/reduce_scatter | solution.py:222
  432.9 1.6 slice.165
  434.5 1.3 slice.164
  (105 shorter events, 24.5 us)
Async XLA Ops:
  7.2 54.7 %copy-start = (f32[128,512]{1,0:T(8,128)S(1)}, f32[128,512]{1,0:T(8,128)}, u32[]{:S(2)}) copy-start(f32[128,512]{1,0:T(8,128)} %param.12) | copy-start | bytes 786436
  7.2 8.3 %collective-permute-start.2 = (bf16[128,1024]{1,0:T(8,128)(2,1)}, bf16[128,1024]{1,0:T(8,128)(2,1)S(1)}, u32[]{:S(2)}, u32[]{:S(2)}) collective-permute-start(bf16[128,1024]{1,0:T(8,128)(2,1)} %param.15), channel_id=1, source_target_pairs={{0,1},{1,2},{2,3},{3,0},{4,5},{5,6},{6,7},{7,4},{8,9},{9,10},{10,1... | collective-permute-start | bytes 786440 | tf_op jit(solution)/shard_map/ppermute | solution.py:147
  8.8 8.5 %collective-permute-start.4 = (bf16[128,1024]{1,0:T(8,128)(2,1)}, bf16[128,1024]{1,0:T(8,128)(2,1)S(1)}, u32[]{:S(2)}, u32[]{:S(2)}) collective-permute-start(bf16[128,1024]{1,0:T(8,128)(2,1)} %param.15), channel_id=1, source_target_pairs={{1,0},{2,1},{3,2},{0,3},{5,4},{6,5},{7,6},{4,7},{9,8},{10,9},{11,1... | collective-permute-start | bytes 786440 | tf_op jit(solution)/shard_map/ppermute | solution.py:149
  10.4 2.2 collective-permute-start
  12.6 11.5 %copy-start.21 = (bf16[128,1024]{1,0:T(8,128)(2,1)S(1)}, bf16[128,1024]{1,0:T(8,128)(2,1)}, u32[]{:S(2)}) copy-start(bf16[128,1024]{1,0:T(8,128)(2,1)} %param.15) | copy-start | bytes 786436
  15.5 8.6 %collective-permute-start.3 = (bf16[128,1024]{1,0:T(8,128)(2,1)S(1)}, bf16[128,1024]{1,0:T(8,128)(2,1)S(1)}, u32[]{:S(2)}, u32[]{:S(2)}) collective-permute-start(bf16[128,1024]{1,0:T(8,128)(2,1)S(1)} %collective-permute-done.2), channel_id=1, source_target_pairs={{0,1},{1,2},{2,3},{3,0},{4,5},{5,6},{6,7},{7,4},{8,9},{9,10},{10,1... | collective-permute-start | bytes 786440 | tf_op jit(solution)/shard_map/ppermute | solution.py:147
  17.3 10.2 %copy-start.8 = (f32[3,128,512]{2,1,0:T(8,128)}, f32[3,128,512]{2,1,0:T(8,128)S(1)}, u32[]{:S(2)}) copy-start(f32[3,128,512]{2,1,0:T(8,128)S(1)} %multiply_add_fusion.3) | copy-start | bytes 2359300
  27.5 4.8 %copy-start.6 = (bf16[128,4,1024]{0,2,1:T(8,128)(2,1)}, bf16[128,4,1024]{0,2,1:T(8,128)(2,1)S(1)}, u32[]{:S(2)}) copy-start(bf16[128,4,1024]{0,2,1:T(8,128)(2,1)S(1)} %copy.50) | copy-start | bytes 3145732
  32.3 6.6 %copy-start.17 = (f32[128,512]{1,0:T(8,128)}, f32[128,512]{1,0:T(8,128)S(1)}, u32[]{:S(2)}) copy-start(f32[128,512]{1,0:T(8,128)S(1)} %get-tuple-element.12) | copy-start | bytes 786436
  32.3 3.2 collective-permute-start.5
  45.1 34.5 %all-to-all-start.2 = ((bf16[64,2,2048]{2,1,0:T(2,128)(2,1)}), bf16[64,2,2048]{2,1,0:T(2,128)(2,1)S(1)}, u32[]{:S(2)}, u32[]{:S(2)}) async-start(bf16[64,2,2048]{2,1,0:T(2,128)(2,1)} %reshape.143), calls=%async_computation.3 | async-start | bytes 1048576 | tf_op jit(solution)/shard_map/all_to_all | solution.py:166
  79.5 0.8 copy-start.14
  80.4 57.2 %all-to-all-start = ((f32[1,256,2048]{2,0,1:T(1,128)}), f32[1,256,2048]{2,0,1:T(1,128)S(1)}, u32[]{:S(2)}, u32[]{:S(2)}) async-start(f32[1,256,2048]{2,0,1:T(1,128)} %copy.44), calls=%async_computation | async-start | bytes 4194304 | tf_op jit(solution)/shard_map/all_to_all | solution.py:112
  152.7 2.4 copy-start.10
  152.7 2.4 copy-start.11
  157.9 3.5 copy-start.4
  164.7 34.4 %all-to-all-start.1 = ((f32[64,4,1024]{2,1,0:T(4,128)}), f32[64,4,1024]{2,1,0:T(4,128)}, u32[]{:S(2)}, u32[]{:S(2)}) async-start(f32[64,4,1024]{2,1,0:T(4,128)} %copy.49), calls=%async_computation.1 | async-start | bytes 2097152 | tf_op jit(solution)/shard_map/all_to_all | solution.py:127
  170.3 1.2 copy-start.3
  170.3 2.8 copy-start.13
  172.3 1.6 copy-start.5
  199.0 34.7 %all-to-all-start.3 = ((bf16[64,4,2048]{2,1,0:T(4,128)(2,1)}), bf16[64,4,2048]{2,1,0:T(4,128)(2,1)S(1)}, u32[]{:S(2)}, u32[]{:S(2)}) async-start(bf16[64,4,2048]{2,1,0:T(4,128)(2,1)} %copy.54), calls=%async_computation.4 | async-start | bytes 2097152 | tf_op jit(solution)/shard_map/all_to_all | solution.py:179
  204.8 64.5 %reduce-scatter.3.cloned.1.call-start = ((), (), s32[]{:S(2)}) async-start(), calls=%async_computation.6 | async-start | bytes 2621440 | tf_op jit(solution)/shard_map/reduce_scatter | solution.py:138
  209.8 0.8 copy-start.15
  209.8 26.9 %copy-start.18 = (f32[128,512]{1,0:T(8,128)S(1)}, f32[128,512]{1,0:T(8,128)}, u32[]{:S(2)}) copy-start(f32[128,512]{1,0:T(8,128)} %copy-done.17) | copy-start | bytes 786436
  209.8 26.9 %copy-start.22 = (f32[512]{0:T(512)S(1)}, f32[512]{0:T(512)}, u32[]{:S(2)}) copy-start(f32[512]{0:T(512)} %param.13) | copy-start | bytes 6148
  210.6 28.0 %copy-start.20 = (f32[128,512]{1,0:T(8,128)S(1)}, f32[128,512]{1,0:T(8,128)}, u32[]{:S(2)}) copy-start(f32[128,512]{1,0:T(8,128)} %get-tuple-element.42) | copy-start | bytes 786436
  210.6 28.0 %collective-permute-start.1 = (f32[128,512]{1,0:T(8,128)S(1)}, f32[128,512]{1,0:T(8,128)}, u32[]{:S(2)}, u32[]{:S(2)}) collective-permute-start(f32[128,512]{1,0:T(8,128)S(1)} %slice.150), channel_id=1, source_target_pairs={{0,4},{4,8},{8,12},{12,16},{16,20},{20,24},{24,28},{28,32},{32,36}... | collective-permute-start | bytes 786440 | tf_op jit(solution)/shard_map/ppermute | solution.py:19
  213.5 25.1 %copy-start.16 = (f32[256,512]{1,0:T(8,128)S(1)}, f32[256,512]{1,0:T(8,128)}, u32[]{:S(2)}) copy-start(f32[256,512]{1,0:T(8,128)} %copy-done.15) | copy-start | bytes 1572868
  234.8 4.8 %copy-start.9 = (f32[3,128,512]{2,1,0:T(8,128)S(1)}, f32[3,128,512]{2,1,0:T(8,128)}, u32[]{:S(2)}) copy-start(f32[3,128,512]{2,1,0:T(8,128)} %copy-done.8) | copy-start | bytes 2359300
  236.7 3.1 copy-start.2
  241.8 1.7 copy-start.7
  241.9 189.7 %reduce-scatter.5.cloned.1.call-start = ((), (), s32[]{:S(2)}) async-start(), calls=%async_computation.7 | async-start | bytes 10649600 | tf_op jit(solution)/shard_map/reduce_scatter | solution.py:222
  242.1 6.0 %collective-permute-start.6 = (f32[3,2,512]{2,1,0:T(2,128)S(1)}, f32[3,2,512]{2,1,0:T(2,128)S(1)}, u32[]{:S(2)}, u32[]{:S(2)}) collective-permute-start(f32[3,2,512]{2,1,0:T(2,128)S(1)} %slice.155), channel_id=1, source_target_pairs={{4,0},{8,4},{12,8},{16,12},{20,16},{24,20},{28,24},{32,28},{36,32}... | collective-permute-start | bytes 36872 | tf_op jit(solution)/shard_map/ppermute | solution.py:19
  259.5 1.2 copy-start.19
  260.8 2.2 copy-start.12
  260.8 175.0 %copy-start.1 = (f32[128,512]{1,0:T(8,128)S(1)}, f32[128,512]{1,0:T(8,128)}, u32[]{:S(2)}) copy-start(f32[128,512]{1,0:T(8,128)} %param.12) | copy-start | bytes 786436
Sparse Core Ops, SparseCore 0:
  242.0 27.3 reduce-scatter.2
  274.2 157.2 reduce-scatter.4
